TPU v7x, 256 devices: a whole 4x4x8 slice. The times are simulated.
256 devices in a mesh: rows: 8 (over y, x_lo), cols: 32 (over z, x_hi, core).
Axes of the slice: x: 4 (x_hi: 2, x_lo: 2; x = x_hi * 2 + x_lo), y: 4, z: 8, core: 2. Of those that a mesh axis runs over, the one named last changes fastest.
Arguments:
- counts: bfloat16 [4096, 262144], P('rows', 'cols'), may hold values from 0 to 12, as said below
- start_a: float32 [4096, 128], P(('rows', 'cols')), may hold values from -0.4 to 0.4
- start_b: float32 [16384, 128], P(('cols', 'rows')), may hold values from -0.4 to 0.4
- start_c: float32 [16, 128], replicated, may hold values from -0.4 to 0.4
Outputs:
- factor_a: float32 [4096, 128], P(('rows', 'cols'))
- factor_b: float32 [16384, 128], P(('cols', 'rows'))
- factor_c: float32 [16, 128], replicated
Inputs may be any that keep to these rules, and one draw needn't show every extreme that they name: counts holds whole numbers.
All inputs are finite; a program needn't handle non-finite values.
Results may differ from a plain program's by a relative error of at most 0.009.
Values may be sent and summed in bfloat16 or wider, within the bound.
No kernel may reach another device: no remote copies, remote signals or barrier semaphores. Data moves between devices by JAX's collectives and lax.ppermute only.
A program may use at most 128 MiB of HBM per device.

v0:
```python
import math
import jax
import jax.numpy as jnp
from jax import lax
from jax.sharding import PartitionSpec as P

ITERS = 2


def local(counts, start_a, start_b, start_c):
    rows_here, flat_width = counts.shape
    depth = start_c.shape[0]
    cols_here = flat_width // depth
    total_i = rows_here * lax.axis_size("rows")
    total_j = cols_here * lax.axis_size("cols")
    rate_a = 0.3 / math.sqrt(total_j * depth)
    rate_b = 0.3 / math.sqrt(total_i * depth)
    rate_c = 0.3 / math.sqrt(total_i * total_j)
    local_a, local_b, shared_c = (start_a, start_b, start_c)
    for iteration in range(ITERS):
        low_a = lax.all_gather(local_a.astype(jnp.bfloat16), "cols", axis=0, tiled=True)
        low_b = lax.all_gather(local_b.astype(jnp.bfloat16), "rows", axis=0, tiled=True)
        low_b_wide = low_b.astype(jnp.float32)
        scaled = (low_b_wide[:, None, :] * shared_c[None, :, :]).astype(jnp.bfloat16)
        scaled = scaled.reshape(cols_here * depth, shared_c.shape[1])
        log_rate = lax.dot_general(
            low_a, scaled, (((1,), (1,)), ((), ())), preferred_element_type=jnp.float32
        )
        residual = (jnp.exp(log_rate) - counts.astype(jnp.float32)).astype(jnp.bfloat16)
        grad_a = jnp.dot(residual, scaled, preferred_element_type=jnp.float32)
        mixed = lax.dot_general(
            residual, low_a, (((0,), (0,)), ((), ())), preferred_element_type=jnp.float32
        )
        mixed = mixed.reshape(cols_here, depth, shared_c.shape[1])
        grad_b = jnp.sum(mixed * shared_c[None, :, :], axis=1)
        grad_c = jnp.sum(mixed * low_b_wide[:, None, :], axis=0)
        summed_a = lax.psum_scatter(grad_a, "cols", scatter_dimension=0, tiled=True)
        summed_b = lax.psum_scatter(grad_b, "rows", scatter_dimension=0, tiled=True)
        local_a = local_a - rate_a * summed_a
        local_b = local_b - rate_b * summed_b
        summed_c = lax.psum(grad_c, ("rows", "cols"))
        shared_c = shared_c - rate_c * summed_c
    return (local_a, local_b, shared_c)


def solution(mesh):
    placed = (P("rows", "cols"), P(("rows", "cols"), None), P(("cols", "rows"), None), P())
    return jax.shard_map(
        local,
        mesh=mesh,
        in_specs=placed,
        out_specs=(P(("rows", "cols"), None), P(("cols", "rows"), None), P()),
        check_vma=False,
    )
```

profile of v0, /device:TPU:32, one launch (start us, length us, event | category | flops | bytes accessed | tf_op | source)
XLA Modules:
  0.0 455.2 jit_solution(1326504930640590621)
XLA Ops:
  7.2 0.0 reduce-scatter.5.cloned.1.call-start
  7.2 12.0 %copy.7 = bf16[512,8192]{0,1:T(8,128)(2,1)} copy(bf16[512,8192]{1,0:T(8,128)(2,1)} %param.4) | data formatting | bytes 16777216 | tf_op args[0]
  19.2 28.6 %all_gather.12 = bf16[512,128]{1,0:T(8,128)(2,1)S(1)} all-gather(bf16[64,128]{1,0:T(8,128)(2,1)S(1)} %convert_element_type.42), channel_id=1, replica_groups=mesh['rows'=8,'cols'=32] {'rows'}, dimensions={0}, use_global_device_ids=true | all-gather | bytes 147456 | tf_op jit(solution)/shard_map/all_gather | solution.py:22
  47.9 42.5 %all_gather.13 = bf16[512,128]{1,0:T(8,128)(2,1)S(1)} all-gather(bf16[16,128]{1,0:T(8,128)(2,1)S(1)} %convert_element_type.46), channel_id=1, replica_groups=mesh['rows'=8,'cols'=32] {'cols'}, dimensions={0}, use_global_device_ids=true | all-gather | bytes 135168 | tf_op jit(solution)/shard_map/all_gather | solution.py:21
  90.4 0.4 multiply_convert_fusion.1
  90.8 5.0 %fusion = bf16[512,8192]{0,1:T(8,128)(2,1)S(1)} fusion(bf16[512,8192]{0,1:T(8,128)(2,1)} %copy.7, bf16[8192,128]{1,0:T(8,128)(2,1)S(1)} %bitcast.22, bf16[512,128]{1,0:T(8,128)(2,1)S(1)} %all_gather.13), kind=kOutput, calls=%fused_computation.2 | convolution fusion | flops 1086324736 | bytes 19005440 | tf_op jit(solution)/shard_map/dot_general | solution.py:26
  95.8 3.2 copy-done
  99.0 3.0 fusion.4
  102.1 0.0 reduce-scatter.7.cloned.1.call-start
  102.1 8.4 %multiply_reduce_fusion.3 = (f32[512,128]{1,0:T(8,128)}, f32[8192,128]{1,0:T(8,128)}) fusion(f32[16,128]{1,0:T(8,128)S(1)} %copy-done.5, bf16[512,8192]{0,1:T(8,128)(2,1)} %copy-done, bf16[512,128]{1,0:T(8,128)(2,1)S(1)} %all_gather.13), kind=kOutput, calls=%fused_computation.8 | convolution fusion | flops 1075773440 | bytes 12984320 | tf_op jit(solution)/shard_map/dot_general | solution.py:31
  110.5 0.0 reduce-scatter.9.cloned.1.call-start
  110.6 2.8 multiply_reduce_fusion.2
  113.4 77.1 %psum.14 = f32[16,128]{1,0:T(8,128)S(1)} all-reduce(f32[16,128]{1,0:T(8,128)S(1)} %multiply_reduce_fusion.2), channel_id=1, replica_groups=mesh['rows'=8,'cols'=32] {'rows','cols'}, use_global_device_ids=true, to_apply=%region_4.0 | all-reduce | flops 2048 | bytes 16384 | tf_op jit(solution)/shard_map/psum | solution.py:41
  190.5 21.8 %reduce-scatter.5.cloned.1.call-done = f32[16,128]{1,0:T(8,128)} async-done(((f32[512,128]{1,0:T(8,128)}), f32[16,128]{1,0:T(8,128)}) %reduce-scatter.5.cloned.1.call-update) | async-done | bytes 8208 | tf_op jit(solution)/shard_map/reduce_scatter | solution.py:37
  212.3 0.7 fusion.3
  213.0 38.0 %all_gather.14 = bf16[512,128]{1,0:T(8,128)(2,1)S(1)} all-gather(bf16[16,128]{1,0:T(8,128)(2,1)S(1)} %fusion.3), channel_id=1, replica_groups=mesh['rows'=8,'cols'=32] {'cols'}, dimensions={0}, use_global_device_ids=true | all-gather | bytes 135168 | tf_op jit(solution)/shard_map/all_gather | solution.py:21
  251.0 2.8 reduce-scatter.7.cloned.1.call-done
  253.8 0.8 fusion.2
  254.6 28.5 %all_gather.15 = bf16[512,128]{1,0:T(8,128)(2,1)S(1)} all-gather(bf16[64,128]{1,0:T(8,128)(2,1)S(1)} %fusion.2), channel_id=1, replica_groups=mesh['rows'=8,'cols'=32] {'rows'}, dimensions={0}, use_global_device_ids=true | all-gather | bytes 147456 | tf_op jit(solution)/shard_map/all_gather | solution.py:22
  283.1 0.4 multiply_convert_fusion
  283.5 5.0 %fusion.1 = bf16[512,8192]{0,1:T(8,128)(2,1)S(1)} fusion(bf16[512,8192]{0,1:T(8,128)(2,1)} %copy.7, bf16[512,128]{1,0:T(8,128)(2,1)S(1)} %all_gather.14, bf16[8192,128]{1,0:T(8,128)(2,1)S(1)} %bitcast.24), kind=kOutput, calls=%fused_computation.3 | convolution fusion | flops 1086324736 | bytes 19005440 | tf_op jit(solution)/shard_map/dot_general | solution.py:26
  288.5 3.2 copy-done.1
  291.7 3.1 fusion.5
  294.8 0.0 reduce-scatter.11.cloned.1.call-start
  294.9 8.4 %multiply_reduce_fusion.1 = (f32[512,128]{1,0:T(8,128)}, f32[8192,128]{1,0:T(8,128)}) fusion(f32[16,128]{1,0:T(8,128)S(1)} %multiply_subtract_fusion.4, bf16[512,8192]{0,1:T(8,128)(2,1)} %copy-done.1, bf16[512,128]{1,0:T(8,128)(2,1)S(1)} %all_gather.14), kind=kOutput, calls=%fused_computation.5 | convolution fusion | flops 1075773440 | bytes 12984320 | tf_op jit(solution)/shard_map/dot_general | solution.py:31
  303.3 2.8 multiply_reduce_fusion
  306.1 73.2 %psum.15 = f32[16,128]{1,0:T(8,128)S(1)} all-reduce(f32[16,128]{1,0:T(8,128)S(1)} %multiply_reduce_fusion), channel_id=1, replica_groups=mesh['rows'=8,'cols'=32] {'rows','cols'}, use_global_device_ids=true, to_apply=%region_9.0 | all-reduce | flops 2048 | bytes 16384 | tf_op jit(solution)/shard_map/psum | solution.py:41
  379.4 0.6 multiply_subtract_fusion.2
  380.0 25.9 %reduce-scatter.9.cloned.1.call-done = f32[16,128]{1,0:T(8,128)} async-done(((f32[512,128]{1,0:T(8,128)}), f32[16,128]{1,0:T(8,128)}) %reduce-scatter.9.cloned.1.call-update) | async-done | bytes 8208 | tf_op jit(solution)/shard_map/reduce_scatter | solution.py:37
  405.9 1.3 multiply_subtract_fusion.3
  407.2 40.1 %reduce-scatter.11.cloned.1.call-done = f32[64,128]{1,0:T(8,128)} async-done(((f32[512,128]{1,0:T(8,128)}), f32[64,128]{1,0:T(8,128)}) %reduce-scatter.11.cloned.1.call-update) | async-done | bytes 32784 | tf_op jit(solution)/shard_map/reduce_scatter | solution.py:38
  447.3 1.4 multiply_subtract_fusion
  (21 shorter events, 0.1 us)
Async XLA Ops:
  7.2 12.0 %copy-start.2 = (f32[64,128]{1,0:T(8,128)S(1)}, f32[64,128]{1,0:T(8,128)}, u32[]{:S(2)}) copy-start(f32[64,128]{1,0:T(8,128)} %param.6) | copy-start | bytes 98308
  7.2 40.7 %copy-start.4 = (f32[16,128]{1,0:T(8,128)S(1)}, f32[16,128]{1,0:T(8,128)}, u32[]{:S(2)}) copy-start(f32[16,128]{1,0:T(8,128)} %param.5) | copy-start | bytes 24580
  7.2 83.2 %copy-start.5 = (f32[16,128]{1,0:T(8,128)S(1)}, f32[16,128]{1,0:T(8,128)}, u32[]{:S(2)}) copy-start(f32[16,128]{1,0:T(8,128)} %param.7) | copy-start | bytes 24580
  7.2 205.1 %reduce-scatter.5.cloned.1.call-start = ((), (), s32[]{:S(2)}) async-start(), calls=%async_computation.4 | async-start | bytes 270336 | tf_op jit(solution)/shard_map/reduce_scatter | solution.py:37
  95.8 3.2 copy-start
  102.1 151.7 %reduce-scatter.7.cloned.1.call-start = ((), (), s32[]{:S(2)}) async-start(), calls=%async_computation.5 | async-start | bytes 294912 | tf_op jit(solution)/shard_map/reduce_scatter | solution.py:38
  110.5 295.3 %reduce-scatter.9.cloned.1.call-start = ((), (), s32[]{:S(2)}) async-start(), calls=%async_computation.6 | async-start | bytes 270336 | tf_op jit(solution)/shard_map/reduce_scatter | solution.py:37
  288.5 3.2 copy-start.1
  294.8 152.5 %reduce-scatter.11.cloned.1.call-start = ((), (), s32[]{:S(2)}) async-start(), calls=%async_computation.7 | async-start | bytes 294912 | tf_op jit(solution)/shard_map/reduce_scatter | solution.py:38
  303.3 102.6 %copy-start.6 = (f32[16,128]{1,0:T(8,128)S(1)}, f32[16,128]{1,0:T(8,128)}, u32[]{:S(2)}) copy-start(f32[16,128]{1,0:T(8,128)} %reduce-scatter.5.cloned.1.call-done) | copy-start | bytes 24580
  303.3 144.0 %copy-start.3 = (f32[64,128]{1,0:T(8,128)S(1)}, f32[64,128]{1,0:T(8,128)}, u32[]{:S(2)}) copy-start(f32[64,128]{1,0:T(8,128)} %reduce-scatter.7.cloned.1.call-done) | copy-start | bytes 98308
Sparse Core Ops, SparseCore 0:
  102.2 110.0 reduce-scatter.4
  214.8 38.9 reduce-scatter.6
  294.9 110.8 reduce-scatter.8
  408.4 38.8 reduce-scatter.10
where the time goes:
time: 456 us; the launch traced here: 455 us
  blocking collectives  288 us (63%)
  waiting for transfers between devices  90.7 us (20%)
  matrix products  33 us (7%)
  local copies, waits for them, and re-layouts  18.4 us (4%)
  between operations  13.9 us (3%)
  other arithmetic  11.1 us (2%)
    psum x2, blocking collectives, local(): summed_c = lax.psum(grad_c, ('rows', 'cols'))  150 us
    all_gather x2, blocking collectives, local(): lax.all_gather(local_a.astype(jnp.bfloat16), 'cols', axis=0, tiled=True)  80.5 us
    all_gather x2, blocking collectives, local(): lax.all_gather(local_b.astype(jnp.bfloat16), 'rows', axis=0, tiled=True)  57.1 us
    reduce_scatter x2, waiting for transfers between devices, local(): summed_a = lax.psum_scatter(grad_a, 'cols', scatter_dimension=0, tiled=True)  47.7 us
    reduce_scatter x2, waiting for transfers between devices, local(): summed_b = lax.psum_scatter(grad_b, 'rows', scatter_dimension=0, tiled=True)  42.9 us
    unnamed x15, local copies, waits for them, and re-layouts  18.4 us
    dot_general x2, matrix products, local(): lax.dot_general(residual, low_a, (((0,), (0,)), ((), ())), preferred_elem...  16.8 us
    dot_general x2, matrix products, local(): lax.dot_general(low_a, scaled, (((1,), (1,)), ((), ())), preferred_elemen...  10.1 us
  transfers between devices with their start and end apart: 4, of which 4 were waited for; matrix products, arithmetic and copies ran while one was open for 5% of the time, Pallas kernels for 0%

commit v1 on v0

--- a/solution.py
+++ b/solution.py
@@ -38,7 +38,7 @@
         summed_b = lax.psum_scatter(grad_b, "rows", scatter_dimension=0, tiled=True)
         local_a = local_a - rate_a * summed_a
         local_b = local_b - rate_b * summed_b
-        summed_c = lax.psum(grad_c, ("rows", "cols"))
+        summed_c = jnp.sum(lax.all_gather(grad_c, ("rows", "cols")), axis=0)
         shared_c = shared_c - rate_c * summed_c
     return (local_a, local_b, shared_c)
 

time: 456 us -> 966 us (2.12)
  waiting for transfers between devices: 90.7 us -> 744 us
  blocking collectives: 288 us -> 138 us
    all_gather x0 -> x2, waiting for transfers between devices: none -> 505 us  [local(): summed_c = jnp.sum(lax.all_gather(grad_c, ('rows', 'cols')), axis=0)]
    psum x2 -> x0, blocking collectives: 150 us -> none  [local(): summed_c = lax.psum(grad_c, ('rows', 'cols'))]
    reduce_scatter x2, waiting for transfers between devices: 47.7 us -> 196 us  [local(): summed_a = lax.psum_scatter(grad_a, 'cols', scatter_dimension=0, tiled=True)]
  transfers between devices with their start and end apart: 4 -> 6, of which waited for: 4 -> 6; matrix products, arithmetic and copies ran while one was open for 5% -> 3% of each run, Pallas kernels for 0% -> 0%
where the time goes in v1:
time: 966 us; the launch traced here: 965 us
  waiting for transfers between devices  744 us (77%)
  blocking collectives  138 us (14%)
  matrix products  33 us (3%)
  local copies, waits for them, and re-layouts  18.4 us (2%)
  other arithmetic  16 us (2%)
  between operations  15.3 us (2%)
    all_gather x2, waiting for transfers between devices, local(): summed_c = jnp.sum(lax.all_gather(grad_c, ('rows', 'cols')), axis=0)  505 us
    reduce_scatter x2, waiting for transfers between devices, local(): summed_a = lax.psum_scatter(grad_a, 'cols', scatter_dimension=0, tiled=True)  196 us
    all_gather x2, blocking collectives, local(): lax.all_gather(local_a.astype(jnp.bfloat16), 'cols', axis=0, tiled=True)  80.6 us
    all_gather x2, blocking collectives, local(): lax.all_gather(local_b.astype(jnp.bfloat16), 'rows', axis=0, tiled=True)  57.2 us
    reduce_scatter x2, waiting for transfers between devices, local(): summed_b = lax.psum_scatter(grad_b, 'rows', scatter_dimension=0, tiled=True)  42.7 us
  transfers between devices with their start and end apart: 6, of which 6 were waited for; matrix products, arithmetic and copies ran while one was open for 3% of the time, Pallas kernels for 0%

profile of v1, /device:TPU:32, one launch (start us, length us, event | category | flops | bytes accessed | tf_op | source)
XLA Modules:
  0.0 964.9 jit_solution(435622260674065794)
XLA Ops:
  8.1 12.0 %copy.9 = bf16[512,8192]{0,1:T(8,128)(2,1)} copy(bf16[512,8192]{1,0:T(8,128)(2,1)} %param.4) | data formatting | bytes 16777216 | tf_op args[0]
  20.0 28.6 %all_gather.24 = bf16[512,128]{1,0:T(8,128)(2,1)S(1)} all-gather(bf16[64,128]{1,0:T(8,128)(2,1)S(1)} %convert_element_type.42), channel_id=1, replica_groups=mesh['rows'=8,'cols'=32] {'rows'}, dimensions={0}, use_global_device_ids=true | all-gather | bytes 147456 | tf_op jit(solution)/shard_map/all_gather | solution.py:22
  48.7 42.5 %all_gather.25 = bf16[512,128]{1,0:T(8,128)(2,1)S(1)} all-gather(bf16[16,128]{1,0:T(8,128)(2,1)S(1)} %convert_element_type.46), channel_id=1, replica_groups=mesh['rows'=8,'cols'=32] {'cols'}, dimensions={0}, use_global_device_ids=true | all-gather | bytes 135168 | tf_op jit(solution)/shard_map/all_gather | solution.py:21
  91.2 0.4 multiply_convert_fusion.1
  91.6 5.0 fusion
  96.7 3.2 copy-done
  99.9 3.0 fusion.4
  103.0 8.4 multiply_reduce_fusion.3
  111.4 0.0 all-gather.5.cloned.1.call-start
  111.4 3.4 multiply_reduce_fusion.2
  114.9 98.4 %reduce-scatter.5.cloned.1.call-done = f32[16,128]{1,0:T(8,128)} async-done(((f32[512,128]{1,0:T(8,128)}), f32[16,128]{1,0:T(8,128)}) %reduce-scatter.5.cloned.1.call-update) | async-done | bytes 8208 | tf_op jit(solution)/shard_map/reduce_scatter | solution.py:37
  213.2 0.7 fusion.3
  213.9 38.1 %all_gather.26 = bf16[512,128]{1,0:T(8,128)(2,1)S(1)} all-gather(bf16[16,128]{1,0:T(8,128)(2,1)S(1)} %fusion.3), channel_id=1, replica_groups=mesh['rows'=8,'cols'=32] {'cols'}, dimensions={0}, use_global_device_ids=true | all-gather | bytes 135168 | tf_op jit(solution)/shard_map/all_gather | solution.py:21
  252.0 2.7 reduce-scatter.7.cloned.1.call-done
  254.7 0.8 fusion.2
  255.5 28.5 %all_gather.27 = bf16[512,128]{1,0:T(8,128)(2,1)S(1)} all-gather(bf16[64,128]{1,0:T(8,128)(2,1)S(1)} %fusion.2), channel_id=1, replica_groups=mesh['rows'=8,'cols'=32] {'rows'}, dimensions={0}, use_global_device_ids=true | all-gather | bytes 147456 | tf_op jit(solution)/shard_map/all_gather | solution.py:22
  284.1 238.4 %all-gather.5.cloned.1.call-done = f32[4096,128]{1,0:T(8,128)} async-done(((f32[16,128]{1,0:T(8,128)}), f32[4096,128]{1,0:T(8,128)}) %all-gather.5.cloned.1.call-update) | async-done | bytes 2097168 | tf_op jit(solution)/shard_map/all_gather | solution.py:41
  522.5 1.9 reduce_sum.56
  524.3 0.4 multiply_convert_fusion
  524.7 5.0 fusion.1
  529.8 3.2 copy-done.1
  533.0 3.1 fusion.5
  536.1 8.4 multiply_reduce_fusion.1
  544.6 0.0 all-gather.7.cloned.1.call-start
  544.6 3.4 multiply_reduce_fusion
  548.0 97.9 %reduce-scatter.9.cloned.1.call-done = f32[16,128]{1,0:T(8,128)} async-done(((f32[512,128]{1,0:T(8,128)}), f32[16,128]{1,0:T(8,128)}) %reduce-scatter.9.cloned.1.call-update) | async-done | bytes 8208 | tf_op jit(solution)/shard_map/reduce_scatter | solution.py:37
  646.0 1.3 multiply_subtract_fusion.3
  647.3 40.0 %reduce-scatter.11.cloned.1.call-done = f32[64,128]{1,0:T(8,128)} async-done(((f32[512,128]{1,0:T(8,128)}), f32[64,128]{1,0:T(8,128)}) %reduce-scatter.11.cloned.1.call-update) | async-done | bytes 32784 | tf_op jit(solution)/shard_map/reduce_scatter | solution.py:38
  687.3 1.4 multiply_subtract_fusion
  688.6 266.7 %all-gather.7.cloned.1.call-done = f32[4096,128]{1,0:T(8,128)} async-done(((f32[16,128]{1,0:T(8,128)}), f32[4096,128]{1,0:T(8,128)}) %all-gather.7.cloned.1.call-update) | async-done | bytes 2097168 | tf_op jit(solution)/shard_map/all_gather | solution.py:41
  955.3 1.9 reduce_sum.59
  957.2 0.6 multiply_subtract_fusion.2
  (27 shorter events, 0.3 us)
Async XLA Ops:
  8.0 12.0 %copy-start.2 = (f32[64,128]{1,0:T(8,128)S(1)}, f32[64,128]{1,0:T(8,128)}, u32[]{:S(2)}) copy-start(f32[64,128]{1,0:T(8,128)} %param.6) | copy-start | bytes 98308
  8.0 40.7 %copy-start.4 = (f32[16,128]{1,0:T(8,128)S(1)}, f32[16,128]{1,0:T(8,128)}, u32[]{:S(2)}) copy-start(f32[16,128]{1,0:T(8,128)} %param.5) | copy-start | bytes 24580
  8.0 83.2 %copy-start.5 = (f32[16,128]{1,0:T(8,128)S(1)}, f32[16,128]{1,0:T(8,128)}, u32[]{:S(2)}) copy-start(f32[16,128]{1,0:T(8,128)} %param.7) | copy-start | bytes 24580
  8.0 205.2 %reduce-scatter.5.cloned.1.call-start = ((), (), s32[]{:S(2)}) async-start(), calls=%async_computation.4 | async-start | bytes 270336 | tf_op jit(solution)/shard_map/reduce_scatter | solution.py:37
  96.6 3.2 copy-start
  102.9 151.8 %reduce-scatter.7.cloned.1.call-start = ((), (), s32[]{:S(2)}) async-start(), calls=%async_computation.5 | async-start | bytes 294912 | tf_op jit(solution)/shard_map/reduce_scatter | solution.py:38
  111.4 411.1 %all-gather.5.cloned.1.call-start = ((), (), s32[]{:S(2)}) async-start(), calls=%async_computation.8 | async-start | bytes 2105344 | tf_op jit(solution)/shard_map/all_gather | solution.py:41
  114.8 531.1 %reduce-scatter.9.cloned.1.call-start = ((), (), s32[]{:S(2)}) async-start(), calls=%async_computation.6 | async-start | bytes 270336 | tf_op jit(solution)/shard_map/reduce_scatter | solution.py:37
  529.8 3.2 copy-start.1
  536.1 151.2 %reduce-scatter.11.cloned.1.call-start = ((), (), s32[]{:S(2)}) async-start(), calls=%async_computation.7 | async-start | bytes 294912 | tf_op jit(solution)/shard_map/reduce_scatter | solution.py:38
  544.5 101.4 %copy-start.6 = (f32[16,128]{1,0:T(8,128)S(1)}, f32[16,128]{1,0:T(8,128)}, u32[]{:S(2)}) copy-start(f32[16,128]{1,0:T(8,128)} %reduce-scatter.5.cloned.1.call-done) | copy-start | bytes 24580
  544.6 142.7 %copy-start.3 = (f32[64,128]{1,0:T(8,128)S(1)}, f32[64,128]{1,0:T(8,128)}, u32[]{:S(2)}) copy-start(f32[64,128]{1,0:T(8,128)} %reduce-scatter.7.cloned.1.call-done) | copy-start | bytes 98308
  544.6 410.7 %all-gather.7.cloned.1.call-start = ((), (), s32[]{:S(2)}) async-start(), calls=%async_computation.9 | async-start | bytes 2105344 | tf_op jit(solution)/shard_map/all_gather | solution.py:41
Sparse Core Ops, SparseCore 0:
  103.0 110.1 reduce-scatter.4
  215.7 38.9 reduce-scatter.6
  536.2 109.7 reduce-scatter.8
  648.5 38.7 reduce-scatter.10
Sparse Core Ops, SparseCore 1:
  114.9 407.5 all-gather.4
  548.1 407.1 all-gather.6
